TPU v7x, 32 devices: a whole 2x2x4 slice. The times are simulated.
32 devices in a mesh: groups: 2 (over x), corpus: 16 (over z, y, core).
Axes of the slice: x: 2, y: 2, z: 4, core: 2. Of those that a mesh axis runs over, the one named last changes fastest.
Arguments:
- queries: bfloat16 [1792, 32, 128], P(('groups', 'corpus')), parts along dimension 0, may hold values from -6 to 6
- passages: bfloat16 [4096, 128, 128], P(('groups', 'corpus')), parts along dimension 0, may hold values from -0.5 to 0.5
- lengths: int32 [4096], P(('groups', 'corpus')), parts along dimension 0, may hold values from 8 to 128
- candidates: int32 [32, 128], P(('groups', 'corpus')), parts along dimension 0, may hold values from 0 to 2047, as said below
Outputs:
- scores: float32 [1792, 128], P(('groups', 'corpus')), parts along dimension 0
- best_scores: float32 [1792, 100], P(('groups', 'corpus')), parts along dimension 0
There are 2 independent parts, one for each index of `groups`. A program takes and returns all parts, laid end to end along the dimension named above; each array names one. Nothing has to cross between parts.
Inputs may be any that keep to these rules, and one draw needn't show every extreme that they name: Row b lists the candidates of queries b * 56 to (b + 1) * 56 - 1. Passage p is held by owner p // 128. In every row at most 12 entries share an owner, and in every row some owner holds exactly 12 of them. Entries may repeat. `lengths`: rows of a tile at or past its length are padding.
All inputs are finite; a program needn't handle non-finite values.
Results may differ from a plain program's by a relative error of at most 0.0003.
Values may be sent and summed in bfloat16 or wider, within the bound.
A program may use at most 128 MiB of HBM per device.

v0:
```python
import math
import jax
import jax.numpy as jnp
from jax import lax
from jax.sharding import PartitionSpec as P

TOPK = 100


def maxsim_many(query_sets, tile_sets, per_device):
    similar = jnp.einsum(
        "srd,sgpd->srgp", query_sets, tile_sets, preferred_element_type=jnp.float32
    )
    nearest = jnp.max(similar, axis=3)
    shards_now = query_sets.shape[0]
    query_tok = query_sets.shape[1] // per_device
    return jnp.sum(
        nearest.reshape(shards_now, per_device, query_tok, nearest.shape[2]), axis=2
    ) / float(query_tok)


def fill_rows(tile_set, tile_len):
    inside = lax.broadcasted_iota(jnp.int32, tile_set.shape[:2], 1) < tile_len[:, None]
    return jnp.where(inside[:, :, None], tile_set, tile_set[:, :1, :])


def local(queries, passages, lengths, candidates):
    peers = lax.axis_size("corpus")
    per_owner, tile_rows, feature = passages.shape
    per_device, query_tok = (queries.shape[0], queries.shape[1])
    candidate_ids = candidates[0]
    number = candidate_ids.shape[0]
    capacity = max(2, 3 * number // (2 * peers))
    owner_of = candidate_ids // per_owner
    local_id = candidate_ids - owner_of * per_owner
    position = jnp.arange(number, dtype=jnp.int32)
    shared = (owner_of[:, None] == owner_of[None, :]) & (position[None, :] < position[:, None])
    rank_in = jnp.sum(shared.astype(jnp.int32), axis=1)
    slot_of = owner_of * capacity + rank_in
    matches = slot_of[None, :] == jnp.arange(peers * capacity, dtype=jnp.int32)[:, None]
    wanted = jnp.max(jnp.where(matches, local_id[None, :], -1), axis=1).reshape(peers, capacity)
    asked = lax.all_to_all(wanted, "corpus", split_axis=0, concat_axis=0, tiled=True)
    picked = jnp.maximum(asked.reshape(-1), 0)
    chosen = fill_rows(passages[picked], lengths[picked])
    by_scorer = chosen.reshape(peers, capacity, tile_rows, feature)
    stacked = queries.reshape(1, per_device * query_tok, feature)
    piece = lax.all_gather(stacked, "corpus", axis=0, tiled=True)
    shards_here = piece.shape[0]
    group_size = math.gcd(shards_here, 8)
    turns = shards_here // group_size
    query_groups = piece.reshape(turns, group_size, piece.shape[1], feature)
    tile_groups = by_scorer.reshape(turns, group_size, capacity, tile_rows, feature)
    fresh_scores = lax.map(
        lambda paired: maxsim_many(paired[0], paired[1], per_device), (query_groups, tile_groups)
    )
    fresh_scores = fresh_scores.reshape(shards_here, per_device, capacity)
    returned = lax.all_to_all(fresh_scores, "corpus", split_axis=0, concat_axis=0, tiled=True)
    spread = jnp.transpose(returned, (1, 0, 2)).reshape(per_device, peers * capacity)
    scores = jnp.take(spread, slot_of, axis=1)
    best_scores = lax.top_k(scores, TOPK)[0]
    return (scores, best_scores)


def solution(mesh):
    return jax.shard_map(
        local,
        mesh=mesh,
        in_specs=(
            P(("groups", "corpus"), None, None),
            P(("groups", "corpus"), None, None),
            P(("groups", "corpus")),
            P(("groups", "corpus"), None),
        ),
        out_specs=(P(("groups", "corpus"), None), P(("groups", "corpus"), None)),
        check_vma=False,
    )
```

profile of v0, /device:TPU:0, one launch (start us, length us, event | category | flops | bytes accessed | tf_op | source)
XLA Modules:
  0.0 137.0 jit_solution(5977993929277204286)
XLA Ops:
  7.2 0.0 copy-start
  7.2 0.0 all-gather.2.cloned.1.call-start
  7.2 0.7 all-gather.2.cloned.1.call-update
  7.9 0.7 subtract_bitcast_fusion
  8.6 0.7 and_select_fusion.2
  9.2 0.2 convert_reduce_fusion
  9.4 0.1 select_reduce_fusion
  9.6 0.7 all_to_all.9
  10.3 7.4 %all-to-all-start = ((s32[16,1,12]{2,1,0:T(1,128)}), s32[16,1,12]{2,1,0:T(1,128)S(1)}, u32[]{:S(2)}, u32[]{:S(2)}) async-start(s32[16,1,12]{2,1,0:T(1,128)} %bitcast.12), calls=%async_computation | async-start | bytes 16384 | tf_op jit(solution)/shard_map/all_to_all | solution.py:42
  17.7 0.7 fusion.6
  18.3 0.7 compare_and_fusion
  19.0 5.0 %all-to-all-done = s32[16,1,12]{2,1,0:T(1,128)S(1)} async-done(((s32[16,1,12]{2,1,0:T(1,128)}), s32[16,1,12]{2,1,0:T(1,128)S(1)}, u32[]{:S(2)}, u32[]{:S(2)}) %all-to-all-start) | async-done | bytes 800 | tf_op jit(solution)/shard_map/all_to_all | solution.py:42
  24.1 0.1 reshape.184
  24.2 10.2 %gather_fusion.1 = bf16[192,128,128]{2,1,0:T(8,128)(2,1)} fusion(bf16[128,128,128]{2,1,0:T(8,128)(2,1)} %param.7, s32[1024]{0:T(1024)S(1)} %pad_clamp_fusion.1), kind=kCustom, calls=%fused_computation.1 | custom fusion | bytes 12583680 | tf_op jit(solution)/shard_map/gather | solution.py:44
  34.3 1.3 slice_reduce_fusion
  35.6 0.0 copy-done
  35.6 1.6 %gather_fusion = s32[192]{0:T(256)S(1)} fusion(s32[128]{0:T(128)S(1)} %copy-done, s32[1024]{0:T(1024)S(1)} %pad_clamp_fusion.1), kind=kCustom, calls=%fused_computation | custom fusion | bytes 2304 | tf_op jit(solution)/shard_map/gather | solution.py:44
  37.2 0.1 lt.53
  37.3 0.1 iota_compare_fusion
  37.4 6.5 %broadcast_select_fusion = bf16[2,8,12,128,128]{4,3,2,1,0:T(8,128)(2,1)} fusion(bf16[2,8,12,128,128]{4,3,2,1,0:T(8,128)(2,1)} %bitcast.73, pred[2,8,12,128]{3,2,1,0:T(8,128)(4,1)S(1)} %iota_compare_fusion, bf16[2,8,12,128]{3,2,1,0:T(8,128)(2,1)S(1)} %broadcast_in_dim.64), kind=kLoop, calls=%fused_computation.10 | loop fusion | flops 3145728 | bytes 12656640 | tf_op jit(solution)/shard_map/jit(_where)/select_n | solution.py:24
  43.9 36.8 %all-gather.2.cloned.1.call-done = bf16[16,1792,128]{2,1,0:T(8,128)(2,1)} async-done(((bf16[1,1792,128]{2,1,0:T(8,128)(2,1)}), bf16[16,1792,128]{2,1,0:T(8,128)(2,1)}) %all-gather.2.cloned.1.call-update) | async-done | bytes 7340048 | tf_op jit(solution)/shard_map/all_gather | solution.py:47
  80.7 32.9 %while.10 = (s32[]{:T(128)}, f32[2,8,56,12]{2,1,0,3:T(8,128)S(1)}, bf16[2,8,1792,128]{3,2,1,0:T(8,128)(2,1)}, bf16[2,8,12,128,128]{4,3,2,1,0:T(8,128)(2,1)}, s32[]{:T(128)}, /*index=5*/f32[]{:T(128)}) while((s32[]{:T(128)}, f32[2,8,56,12]{2,1,0,3:T(8,128)S(1)}, bf16[2,8,1792,128]{3,2,1,0:T(8,128)(2,1)}, ...), condition=%wide.region_5.6_spmd, body=%wide.region_2.5_spmd.sunk | while | flops 5659164672 | bytes 11065421 | solution.py:53
  80.7 14.4 %convolution_reduce_fusion.2 = f32[8,1792,12]{1,2,0:T(8,128)S(1)} fusion(bf16[2,8,1792,128]{3,2,1,0:T(8,128)(2,1)} %get-tuple-element.87, s32[]{:T(128)} %get-tuple-element.79, bf16[2,8,12,128,128]{4,3,2,1,0:T(8,128)(2,1)} %get-tuple-element.88), kind=kOutput, calls=%fused_computation.3.clone.1 | convolution fusion | flops 5658992640 | bytes 7504896 | tf_op jit(solution)/shard_map/while/body/eval_jaxpr/srd,sgpd->srgp/dot_general | solution.py:11
  95.1 0.4 copy.35
  95.5 0.8 reshape.220
  96.4 0.8 reduce_sum.27
  97.2 14.4 %convolution_reduce_fusion.2 = f32[8,1792,12]{1,2,0:T(8,128)S(1)} fusion(bf16[2,8,1792,128]{3,2,1,0:T(8,128)(2,1)} %get-tuple-element.87, s32[]{:T(128)} %get-tuple-element.79, bf16[2,8,12,128,128]{4,3,2,1,0:T(8,128)(2,1)} %get-tuple-element.88), kind=kOutput, calls=%fused_computation.3.clone.1 | convolution fusion | flops 5658992640 | bytes 7504896 | tf_op jit(solution)/shard_map/while/body/eval_jaxpr/srd,sgpd->srgp/dot_general | solution.py:11
  111.6 0.4 copy.35
  112.0 0.8 reshape.220
  112.8 0.8 reduce_sum.27
  113.7 0.8 reshape.217
  114.5 3.5 %all-to-all-start.1 = ((f32[16,1,672]{2,1,0:T(1,128)}), f32[16,1,672]{2,1,0:T(1,128)S(1)}, u32[]{:S(2)}, u32[]{:S(2)}) async-start(f32[16,1,672]{2,1,0:T(1,128)} %reshape.217), calls=%async_computation.1 | async-start | bytes 98304 | tf_op jit(solution)/shard_map/all_to_all | solution.py:57
  118.0 6.7 %all-to-all-done.1 = f32[16,1,672]{2,1,0:T(1,128)S(1)} async-done(((f32[16,1,672]{2,1,0:T(1,128)}), f32[16,1,672]{2,1,0:T(1,128)S(1)}, u32[]{:S(2)}, u32[]{:S(2)}) %all-to-all-start.1) | async-done | bytes 43040 | tf_op jit(solution)/shard_map/all_to_all | solution.py:57
  124.7 0.5 broadcast.219
  125.2 0.8 reduce.6
  126.0 0.1 reshape.218
  126.1 0.6 gather_fusion.2
  126.8 0.1 select_bitcast_fusion
  126.9 0.1 copy.27
  126.9 0.0 copy-start.1
  126.9 3.2 %top_k.9 = (f32[56,128]{1,0:T(8,128)}, s32[56,128]{1,0:T(8,128)}) sort(f32[56,128]{1,0:T(8,128)S(1)} %copy.27, s32[56,128]{1,0:T(8,128)S(1)} %iota.22), dimensions={1}, to_apply=%region_6.7 | sort | flops 93184 | bytes 114688 | tf_op jit(solution)/shard_map/top_k | solution.py:60
  130.1 0.0 copy-done.1
  (12 shorter events, 0.1 us)
Async XLA Ops:
  7.2 28.5 %copy-start = (s32[128]{0:T(128)S(1)}, s32[128]{0:T(128)}, u32[]{:S(2)}) copy-start(s32[128]{0:T(128)} %param.8) | copy-start | bytes 1540
  7.2 73.5 %all-gather.2.cloned.1.call-start = ((), (), s32[]{:S(2)}) async-start(), calls=%async_computation.2 | async-start | bytes 7798784 | tf_op jit(solution)/shard_map/all_gather | solution.py:47
  10.3 13.8 %all-to-all-start = ((s32[16,1,12]{2,1,0:T(1,128)}), s32[16,1,12]{2,1,0:T(1,128)S(1)}, u32[]{:S(2)}, u32[]{:S(2)}) async-start(s32[16,1,12]{2,1,0:T(1,128)} %bitcast.12), calls=%async_computation | async-start | bytes 16384 | tf_op jit(solution)/shard_map/all_to_all | solution.py:42
  114.5 10.2 %all-to-all-start.1 = ((f32[16,1,672]{2,1,0:T(1,128)}), f32[16,1,672]{2,1,0:T(1,128)S(1)}, u32[]{:S(2)}, u32[]{:S(2)}) async-start(f32[16,1,672]{2,1,0:T(1,128)} %reshape.217), calls=%async_computation.1 | async-start | bytes 98304 | tf_op jit(solution)/shard_map/all_to_all | solution.py:57
  126.9 3.2 %copy-start.1 = (f32[56,128]{1,0:T(8,128)}, f32[56,128]{1,0:T(8,128)S(1)}, u32[]{:S(2)}) copy-start(f32[56,128]{1,0:T(8,128)S(1)} %copy.27) | copy-start | bytes 86020
Sparse Core Ops, SparseCore 0:
  10.3 70.3 all-gather.1
where the time goes:
time: 137 us
  waiting for transfers between devices  49.2 us (36%)
  matrix products  28.8 us (21%)
  local copies, waits for them, and re-layouts  18.4 us (13%)
  other arithmetic  15.3 us (11%)
  between operations  14.2 us (10%)
  starting transfers between devices  10.9 us (8%)
    all_gather x1, waiting for transfers between devices, local(): piece = lax.all_gather(stacked, 'corpus', axis=0, tiled=True)  36.8 us
    dot_general x2, matrix products, maxsim_many(): jnp.einsum('srd,sgpd->srgp', query_sets, tile_sets, preferred_element_typ...  28.8 us
    gather x2, local copies, waits for them, and re-layouts, local(): chosen = fill_rows(passages[picked], lengths[picked])  11.7 us
    all_to_all x1, starting transfers between devices, local(): lax.all_to_all(wanted, 'corpus', split_axis=0, concat_axis=0, tiled=True)  7.41 us
    all_to_all x1, waiting for transfers between devices, local(): lax.all_to_all(fresh_scores, 'corpus', split_axis=0, concat_axis=0, tiled...  6.72 us
    select_n x1, other arithmetic, fill_rows(): return jnp.where(inside[:, :, None], tile_set, tile_set[:, :1, :])  6.55 us
    all_to_all x1, waiting for transfers between devices, local(): lax.all_to_all(wanted, 'corpus', split_axis=0, concat_axis=0, tiled=True)  5.01 us
    all_to_all x1, starting transfers between devices, local(): lax.all_to_all(fresh_scores, 'corpus', split_axis=0, concat_axis=0, tiled...  3.5 us
  transfers between devices with their start and end apart: 3, of which 3 were waited for; matrix products, arithmetic and copies ran while one was open for 17% of the time, Pallas kernels for 0%

commit v1 on v0

--- a/solution.py
+++ b/solution.py
@@ -44,7 +44,14 @@
     chosen = fill_rows(passages[picked], lengths[picked])
     by_scorer = chosen.reshape(peers, capacity, tile_rows, feature)
     stacked = queries.reshape(1, per_device * query_tok, feature)
-    piece = lax.all_gather(stacked, "corpus", axis=0, tiled=True)
+    ring = [stacked]
+    for hop in range(15):
+        ring.append(lax.ppermute(ring[-1], "corpus", [(dev, (dev + 1) % 16) for dev in range(16)]))
+    piece = jnp.roll(
+        jnp.concatenate(ring[::-1], axis=0),
+        (lax.axis_index("corpus") + 1) * ring[0].shape[0],
+        axis=0,
+    )
     shards_here = piece.shape[0]
     group_size = math.gcd(shards_here, 8)
     turns = shards_here // group_size

time: 137 us -> 257 us (1.88)
  waiting for transfers between devices: 49.2 us -> 142 us
  local copies, waits for them, and re-layouts: 18.4 us -> 59.2 us
  between operations: 14.2 us -> 0.94 us
    ppermute x0 -> x15, waiting for transfers between devices: none -> 130 us  [local(): lax.ppermute(ring[-1], 'corpus', [(dev, (dev + 1) % 16) for dev in range(...]
    all_gather x1 -> x0, waiting for transfers between devices: 36.8 us -> none  [local(): piece = lax.all_gather(stacked, 'corpus', axis=0, tiled=True)]
    unnamed x7 -> x66, local copies, waits for them, and re-layouts: 0.95 us -> 34.1 us
    dynamic_slice x0 -> x1, local copies, waits for them, and re-layouts: none -> 6.73 us  [local(): jnp.roll(jnp.concatenate(ring[::-1], axis=0), (lax.axis_index('corpus') +...]
  transfers between devices with their start and end apart: 3 -> 17, of which waited for: 3 -> 15; matrix products, arithmetic and copies ran while one was open for 17% -> 9% of each run, Pallas kernels for 0% -> 0%
where the time goes in v1:
time: 257 us
  waiting for transfers between devices  142 us (55%)
  local copies, waits for them, and re-layouts  59.2 us (23%)
  matrix products  28.8 us (11%)
  other arithmetic  14.5 us (6%)
  starting transfers between devices  10.8 us (4%)
    ppermute x15, waiting for transfers between devices, local(): lax.ppermute(ring[-1], 'corpus', [(dev, (dev + 1) % 16) for dev in range(...  130 us
    unnamed x66, local copies, waits for them, and re-layouts  34.1 us
    dot_general x2, matrix products, maxsim_many(): jnp.einsum('srd,sgpd->srgp', query_sets, tile_sets, preferred_element_typ...  28.8 us
    gather x2, local copies, waits for them, and re-layouts, local(): chosen = fill_rows(passages[picked], lengths[picked])  11.8 us
    dynamic_slice x1, local copies, waits for them, and re-layouts, local(): jnp.roll(jnp.concatenate(ring[::-1], axis=0), (lax.axis_index('corpus') +...  6.73 us
    all_to_all x1, waiting for transfers between devices, local(): lax.all_to_all(fresh_scores, 'corpus', split_axis=0, concat_axis=0, tiled...  6.7 us
    select_n x1, other arithmetic, fill_rows(): return jnp.where(inside[:, :, None], tile_set, tile_set[:, :1, :])  6.51 us
    all_to_all x1, starting transfers between devices, local(): lax.all_to_all(wanted, 'corpus', split_axis=0, concat_axis=0, tiled=True)  5.82 us
  transfers between devices with their start and end apart: 17, of which 15 were waited for; matrix products, arithmetic and copies ran while one was open for 9% of the time, Pallas kernels for 0%

profile of v1, /device:TPU:0, one launch (start us, length us, event | category | flops | bytes accessed | tf_op | source)
XLA Modules:
  0.0 256.9 jit_solution(14145084762843627252)
XLA Ops:
  1.2 11.4 %collective-permute-done = bf16[1,1792,128]{2,1,0:T(8,128)(2,1)S(1)} collective-permute-done((bf16[1,1792,128]{2,1,0:T(8,128)(2,1)}, bf16[1,1792,128]{2,1,0:T(8,128)(2,1)S(1)}, u32[]{:S(2)}, u32[]{:S(2)}) %collective-permute-start) | collective-permute-done | bytes 458784 | tf_op jit(solution)/shard_map/ppermute | solution.py:49
  12.6 10.6 %collective-permute-done.1 = bf16[1,1792,128]{2,1,0:T(8,128)(2,1)S(1)} collective-permute-done((bf16[1,1792,128]{2,1,0:T(8,128)(2,1)S(1)}, bf16[1,1792,128]{2,1,0:T(8,128)(2,1)S(1)}, u32[]{:S(2)}, u32[]{:S(2)}) %collective-permute-start.1) | collective-permute-done | bytes 458784 | tf_op jit(solution)/shard_map/ppermute | solution.py:49
  23.2 10.6 %collective-permute-done.2 = bf16[1,1792,128]{2,1,0:T(8,128)(2,1)S(1)} collective-permute-done((bf16[1,1792,128]{2,1,0:T(8,128)(2,1)S(1)}, bf16[1,1792,128]{2,1,0:T(8,128)(2,1)S(1)}, u32[]{:S(2)}, u32[]{:S(2)}) %collective-permute-start.2) | collective-permute-done | bytes 458784 | tf_op jit(solution)/shard_map/ppermute | solution.py:49
  33.8 10.6 %collective-permute-done.3 = bf16[1,1792,128]{2,1,0:T(8,128)(2,1)S(1)} collective-permute-done((bf16[1,1792,128]{2,1,0:T(8,128)(2,1)S(1)}, bf16[1,1792,128]{2,1,0:T(8,128)(2,1)S(1)}, u32[]{:S(2)}, u32[]{:S(2)}) %collective-permute-start.3) | collective-permute-done | bytes 458784 | tf_op jit(solution)/shard_map/ppermute | solution.py:49
  44.4 10.6 %collective-permute-done.4 = bf16[1,1792,128]{2,1,0:T(8,128)(2,1)S(1)} collective-permute-done((bf16[1,1792,128]{2,1,0:T(8,128)(2,1)S(1)}, bf16[1,1792,128]{2,1,0:T(8,128)(2,1)S(1)}, u32[]{:S(2)}, u32[]{:S(2)}) %collective-permute-start.4) | collective-permute-done | bytes 458784 | tf_op jit(solution)/shard_map/ppermute | solution.py:49
  55.0 10.6 %collective-permute-done.5 = bf16[1,1792,128]{2,1,0:T(8,128)(2,1)S(1)} collective-permute-done((bf16[1,1792,128]{2,1,0:T(8,128)(2,1)S(1)}, bf16[1,1792,128]{2,1,0:T(8,128)(2,1)S(1)}, u32[]{:S(2)}, u32[]{:S(2)}) %collective-permute-start.5) | collective-permute-done | bytes 458784 | tf_op jit(solution)/shard_map/ppermute | solution.py:49
  65.6 10.6 %collective-permute-done.6 = bf16[1,1792,128]{2,1,0:T(8,128)(2,1)S(1)} collective-permute-done((bf16[1,1792,128]{2,1,0:T(8,128)(2,1)S(1)}, bf16[1,1792,128]{2,1,0:T(8,128)(2,1)S(1)}, u32[]{:S(2)}, u32[]{:S(2)}) %collective-permute-start.6) | collective-permute-done | bytes 458784 | tf_op jit(solution)/shard_map/ppermute | solution.py:49
  76.2 0.8 copy-done.2
  77.0 10.6 %collective-permute-done.7 = bf16[1,1792,128]{2,1,0:T(8,128)(2,1)S(1)} collective-permute-done((bf16[1,1792,128]{2,1,0:T(8,128)(2,1)S(1)}, bf16[1,1792,128]{2,1,0:T(8,128)(2,1)S(1)}, u32[]{:S(2)}, u32[]{:S(2)}) %collective-permute-start.7) | collective-permute-done | bytes 458784 | tf_op jit(solution)/shard_map/ppermute | solution.py:49
  87.6 0.8 copy-done.4
  88.3 10.6 %collective-permute-done.8 = bf16[1,1792,128]{2,1,0:T(8,128)(2,1)S(1)} collective-permute-done((bf16[1,1792,128]{2,1,0:T(8,128)(2,1)S(1)}, bf16[1,1792,128]{2,1,0:T(8,128)(2,1)S(1)}, u32[]{:S(2)}, u32[]{:S(2)}) %collective-permute-start.8) | collective-permute-done | bytes 458784 | tf_op jit(solution)/shard_map/ppermute | solution.py:49
  99.7 10.6 %collective-permute-done.9 = bf16[1,1792,128]{2,1,0:T(8,128)(2,1)S(1)} collective-permute-done((bf16[1,1792,128]{2,1,0:T(8,128)(2,1)S(1)}, bf16[1,1792,128]{2,1,0:T(8,128)(2,1)S(1)}, u32[]{:S(2)}, u32[]{:S(2)}) %collective-permute-start.9) | collective-permute-done | bytes 458784 | tf_op jit(solution)/shard_map/ppermute | solution.py:49
  111.1 10.6 %collective-permute-done.10 = bf16[1,1792,128]{2,1,0:T(8,128)(2,1)S(1)} collective-permute-done((bf16[1,1792,128]{2,1,0:T(8,128)(2,1)S(1)}, bf16[1,1792,128]{2,1,0:T(8,128)(2,1)S(1)}, u32[]{:S(2)}, u32[]{:S(2)}) %collective-permute-start.10) | collective-permute-done | bytes 458784 | tf_op jit(solution)/shard_map/ppermute | solution.py:49
  124.0 9.1 %collective-permute-done.11 = bf16[1,1792,128]{2,1,0:T(8,128)(2,1)S(1)} collective-permute-done((bf16[1,1792,128]{2,1,0:T(8,128)(2,1)S(1)}, bf16[1,1792,128]{2,1,0:T(8,128)(2,1)S(1)}, u32[]{:S(2)}, u32[]{:S(2)}) %collective-permute-start.11) | collective-permute-done | bytes 458784 | tf_op jit(solution)/shard_map/ppermute | solution.py:49
  133.9 5.8 %all-to-all-start = ((s32[16,1,12]{2,1,0:T(1,128)}), s32[16,1,12]{2,1,0:T(1,128)S(1)}, u32[]{:S(2)}, u32[]{:S(2)}) async-start(s32[16,1,12]{2,1,0:T(1,128)} %bitcast.12), calls=%async_computation | async-start | bytes 16384 | tf_op jit(solution)/shard_map/all_to_all | solution.py:42
  140.4 5.7 %all-to-all-done = s32[16,1,12]{2,1,0:T(1,128)S(1)} async-done(((s32[16,1,12]{2,1,0:T(1,128)}), s32[16,1,12]{2,1,0:T(1,128)S(1)}, u32[]{:S(2)}, u32[]{:S(2)}) %all-to-all-start) | async-done | bytes 800 | tf_op jit(solution)/shard_map/all_to_all | solution.py:42
  146.3 10.2 %gather_fusion.1 = bf16[192,128,128]{2,1,0:T(8,128)(2,1)} fusion(bf16[128,128,128]{2,1,0:T(8,128)(2,1)} %param.7, s32[1024]{0:T(1024)S(1)} %get-tuple-element.49), kind=kCustom, calls=%fused_computation.1 | custom fusion | bytes 12583680 | tf_op jit(solution)/shard_map/gather | solution.py:44
  156.5 1.3 slice_reduce_fusion
  157.9 1.6 gather_fusion
  159.7 0.9 collective-permute-start.14
  160.5 6.5 %broadcast_select_fusion = bf16[2,8,12,128,128]{4,3,2,1,0:T(8,128)(2,1)} fusion(bf16[2,8,12,128,128]{4,3,2,1,0:T(8,128)(2,1)} %bitcast.77, pred[2,8,12,128]{3,2,1,0:T(8,128)(4,1)S(1)} %iota_compare_fusion, bf16[2,8,12,128]{3,2,1,0:T(8,128)(2,1)S(1)} %broadcast_in_dim.64), kind=kLoop, calls=%fused_computation.10 | loop fusion | flops 3145728 | bytes 12656640 | tf_op jit(solution)/shard_map/jit(_where)/select_n | solution.py:24
  167.1 3.7 %collective-permute-done.14 = bf16[1,1792,128]{2,1,0:T(8,128)(2,1)S(1)} collective-permute-done((bf16[1,1792,128]{2,1,0:T(8,128)(2,1)}, bf16[1,1792,128]{2,1,0:T(8,128)(2,1)S(1)}, u32[]{:S(2)}, u32[]{:S(2)}) %collective-permute-start.14) | collective-permute-done | bytes 458784 | tf_op jit(solution)/shard_map/ppermute | solution.py:49
  170.7 0.8 constant_dynamic-update-slice_fusion.31
  171.5 1.8 constant_dynamic-update-slice_fusion.30
  173.4 1.8 constant_dynamic-update-slice_fusion.29
  175.2 0.8 constant_dynamic-update-slice_fusion.28
  176.0 0.8 constant_dynamic-update-slice_fusion.27
  176.8 0.8 constant_dynamic-update-slice_fusion.26
  177.6 0.8 constant_dynamic-update-slice_fusion.25
  178.5 0.8 constant_dynamic-update-slice_fusion.24
  179.3 0.8 constant_dynamic-update-slice_fusion.23
  180.1 0.8 constant_dynamic-update-slice_fusion.22
  180.9 0.8 constant_dynamic-update-slice_fusion.21
  181.7 0.8 constant_dynamic-update-slice_fusion.20
  182.5 0.8 constant_dynamic-update-slice_fusion.19
  183.3 0.8 constant_dynamic-update-slice_fusion.18
  184.1 0.8 constant_dynamic-update-slice_fusion.17
  184.9 0.8 constant_dynamic-update-slice_fusion.16
  185.7 0.8 constant_dynamic-update-slice_fusion.15
  186.5 1.8 constant_dynamic-update-slice_fusion.14
  188.3 1.9 constant_dynamic-update-slice_fusion.13
  190.2 0.8 constant_dynamic-update-slice_fusion.12
  191.1 0.8 constant_dynamic-update-slice_fusion.11
  191.9 0.8 constant_dynamic-update-slice_fusion.10
  192.7 0.8 constant_dynamic-update-slice_fusion.9
  193.5 0.8 constant_dynamic-update-slice_fusion.8
  194.3 0.8 constant_dynamic-update-slice_fusion.7
  195.1 0.8 constant_dynamic-update-slice_fusion.6
  195.9 0.8 constant_dynamic-update-slice_fusion.5
  196.7 0.8 constant_dynamic-update-slice_fusion.4
  197.5 0.8 constant_dynamic-update-slice_fusion.3
  198.3 0.8 constant_dynamic-update-slice_fusion.2
  199.2 0.8 constant_dynamic-update-slice_fusion.1
  199.9 0.8 constant_dynamic-update-slice_fusion
  200.8 6.7 %constant_dynamic-slice_fusion = bf16[16,1792,128]{2,1,0:T(8,128)(2,1)} fusion(bf16[32,1792,128]{2,1,0:T(8,128)(2,1)} %constant_dynamic-update-slice_fusion, s32[]{:T(128)S(6)} %select_n.71), kind=kLoop, calls=%fused_computation.76 | loop fusion | bytes 14680068 | tf_op jit(solution)/shard_map/jit(_roll_dynamic)/dynamic_slice | solution.py:50
  207.5 32.9 %while.10 = (s32[]{:T(128)}, f32[2,8,56,12]{2,1,0,3:T(8,128)S(1)}, bf16[2,8,1792,128]{3,2,1,0:T(8,128)(2,1)}, bf16[2,8,12,128,128]{4,3,2,1,0:T(8,128)(2,1)}, s32[]{:T(128)}, /*index=5*/f32[]{:T(128)}) while((s32[]{:T(128)}, f32[2,8,56,12]{2,1,0,3:T(8,128)S(1)}, bf16[2,8,1792,128]{3,2,1,0:T(8,128)(2,1)}, ...), condition=%wide.region_5.6_spmd, body=%wide.region_2.5_spmd.sunk | while | flops 5659164672 | bytes 11065421 | solution.py:60
  207.5 14.4 %convolution_reduce_fusion.2 = f32[8,1792,12]{1,2,0:T(8,128)S(1)} fusion(bf16[2,8,1792,128]{3,2,1,0:T(8,128)(2,1)} %get-tuple-element.89, s32[]{:T(128)} %get-tuple-element.81, bf16[2,8,12,128,128]{4,3,2,1,0:T(8,128)(2,1)} %get-tuple-element.90), kind=kOutput, calls=%fused_computation.3.clone.1 | convolution fusion | flops 5658992640 | bytes 7504896 | tf_op jit(solution)/shard_map/while/body/eval_jaxpr/srd,sgpd->srgp/dot_general | solution.py:11
  222.3 0.8 reshape.220
  223.1 0.8 reduce_sum.27
  224.0 14.4 %convolution_reduce_fusion.2 = f32[8,1792,12]{1,2,0:T(8,128)S(1)} fusion(bf16[2,8,1792,128]{3,2,1,0:T(8,128)(2,1)} %get-tuple-element.89, s32[]{:T(128)} %get-tuple-element.81, bf16[2,8,12,128,128]{4,3,2,1,0:T(8,128)(2,1)} %get-tuple-element.90), kind=kOutput, calls=%fused_computation.3.clone.1 | convolution fusion | flops 5658992640 | bytes 7504896 | tf_op jit(solution)/shard_map/while/body/eval_jaxpr/srd,sgpd->srgp/dot_general | solution.py:11
  238.8 0.8 reshape.220
  241.2 3.5 %all-to-all-start.1 = ((f32[16,1,672]{2,1,0:T(1,128)}), f32[16,1,672]{2,1,0:T(1,128)S(1)}, u32[]{:S(2)}, u32[]{:S(2)}) async-start(f32[16,1,672]{2,1,0:T(1,128)} %reshape.217), calls=%async_computation.1 | async-start | bytes 98304 | tf_op jit(solution)/shard_map/all_to_all | solution.py:64
  244.8 6.7 %all-to-all-done.1 = f32[16,1,672]{2,1,0:T(1,128)S(1)} async-done(((f32[16,1,672]{2,1,0:T(1,128)}), f32[16,1,672]{2,1,0:T(1,128)S(1)}, u32[]{:S(2)}, u32[]{:S(2)}) %all-to-all-start.1) | async-done | bytes 43040 | tf_op jit(solution)/shard_map/all_to_all | solution.py:64
  253.7 3.2 %top_k.9 = (f32[56,128]{1,0:T(8,128)}, s32[56,128]{1,0:T(8,128)}) sort(f32[56,128]{1,0:T(8,128)S(1)} %copy.27, s32[56,128]{1,0:T(8,128)S(1)} %iota.22), dimensions={1}, to_apply=%region_6.7 | sort | flops 93184 | bytes 114688 | tf_op jit(solution)/shard_map/top_k | solution.py:67
  (77 shorter events, 10.9 us)
Async XLA Ops:
  0.6 157.2 %copy-start = (s32[128]{0:T(128)S(1)}, s32[128]{0:T(128)}, u32[]{:S(2)}) copy-start(s32[128]{0:T(128)} %param.8) | copy-start | bytes 1540
  0.6 11.9 %collective-permute-start = (bf16[1,1792,128]{2,1,0:T(8,128)(2,1)}, bf16[1,1792,128]{2,1,0:T(8,128)(2,1)S(1)}, u32[]{:S(2)}, u32[]{:S(2)}) collective-permute-start(bf16[1,1792,128]{2,1,0:T(8,128)(2,1)} %bitcast.79), channel_id=1, source_target_pairs={{0,1},{1,2},{2,3},{3,4},{4,5},{5,6},{6,7},{7,8},{8,9},{9,10},{10,1... | collective-permute-start | bytes 1376264 | tf_op jit(solution)/shard_map/ppermute | solution.py:49
  12.5 10.6 %collective-permute-start.1 = (bf16[1,1792,128]{2,1,0:T(8,128)(2,1)S(1)}, bf16[1,1792,128]{2,1,0:T(8,128)(2,1)S(1)}, u32[]{:S(2)}, u32[]{:S(2)}) collective-permute-start(bf16[1,1792,128]{2,1,0:T(8,128)(2,1)S(1)} %collective-permute-done), channel_id=1, source_target_pairs={{0,1},{1,2},{2,3},{3,4},{4,5},{5,6},{6,7},{7,8},{8,9},{9,10},{10,1... | collective-permute-start | bytes 1376264 | tf_op jit(solution)/shard_map/ppermute | solution.py:49
  23.1 10.6 %collective-permute-start.2 = (bf16[1,1792,128]{2,1,0:T(8,128)(2,1)S(1)}, bf16[1,1792,128]{2,1,0:T(8,128)(2,1)S(1)}, u32[]{:S(2)}, u32[]{:S(2)}) collective-permute-start(bf16[1,1792,128]{2,1,0:T(8,128)(2,1)S(1)} %collective-permute-done.1), channel_id=1, source_target_pairs={{0,1},{1,2},{2,3},{3,4},{4,5},{5,6},{6,7},{7,8},{8,9},{9,10},{10,1... | collective-permute-start | bytes 1376264 | tf_op jit(solution)/shard_map/ppermute | solution.py:49
  33.8 10.6 %collective-permute-start.3 = (bf16[1,1792,128]{2,1,0:T(8,128)(2,1)S(1)}, bf16[1,1792,128]{2,1,0:T(8,128)(2,1)S(1)}, u32[]{:S(2)}, u32[]{:S(2)}) collective-permute-start(bf16[1,1792,128]{2,1,0:T(8,128)(2,1)S(1)} %collective-permute-done.2), channel_id=1, source_target_pairs={{0,1},{1,2},{2,3},{3,4},{4,5},{5,6},{6,7},{7,8},{8,9},{9,10},{10,1... | collective-permute-start | bytes 1376264 | tf_op jit(solution)/shard_map/ppermute | solution.py:49
  44.4 10.6 %collective-permute-start.4 = (bf16[1,1792,128]{2,1,0:T(8,128)(2,1)S(1)}, bf16[1,1792,128]{2,1,0:T(8,128)(2,1)S(1)}, u32[]{:S(2)}, u32[]{:S(2)}) collective-permute-start(bf16[1,1792,128]{2,1,0:T(8,128)(2,1)S(1)} %collective-permute-done.3), channel_id=1, source_target_pairs={{0,1},{1,2},{2,3},{3,4},{4,5},{5,6},{6,7},{7,8},{8,9},{9,10},{10,1... | collective-permute-start | bytes 1376264 | tf_op jit(solution)/shard_map/ppermute | solution.py:49
  55.0 10.6 %collective-permute-start.5 = (bf16[1,1792,128]{2,1,0:T(8,128)(2,1)S(1)}, bf16[1,1792,128]{2,1,0:T(8,128)(2,1)S(1)}, u32[]{:S(2)}, u32[]{:S(2)}) collective-permute-start(bf16[1,1792,128]{2,1,0:T(8,128)(2,1)S(1)} %collective-permute-done.4), channel_id=1, source_target_pairs={{0,1},{1,2},{2,3},{3,4},{4,5},{5,6},{6,7},{7,8},{8,9},{9,10},{10,1... | collective-permute-start | bytes 1376264 | tf_op jit(solution)/shard_map/ppermute | solution.py:49
  65.6 10.6 %collective-permute-start.6 = (bf16[1,1792,128]{2,1,0:T(8,128)(2,1)S(1)}, bf16[1,1792,128]{2,1,0:T(8,128)(2,1)S(1)}, u32[]{:S(2)}, u32[]{:S(2)}) collective-permute-start(bf16[1,1792,128]{2,1,0:T(8,128)(2,1)S(1)} %collective-permute-done.5), channel_id=1, source_target_pairs={{0,1},{1,2},{2,3},{3,4},{4,5},{5,6},{6,7},{7,8},{8,9},{9,10},{10,1... | collective-permute-start | bytes 1376264 | tf_op jit(solution)/shard_map/ppermute | solution.py:49
  76.2 0.8 copy-start.2
  77.0 10.6 %collective-permute-start.7 = (bf16[1,1792,128]{2,1,0:T(8,128)(2,1)S(1)}, bf16[1,1792,128]{2,1,0:T(8,128)(2,1)S(1)}, u32[]{:S(2)}, u32[]{:S(2)}) collective-permute-start(bf16[1,1792,128]{2,1,0:T(8,128)(2,1)S(1)} %collective-permute-done.6), channel_id=1, source_target_pairs={{0,1},{1,2},{2,3},{3,4},{4,5},{5,6},{6,7},{7,8},{8,9},{9,10},{10,1... | collective-permute-start | bytes 1376264 | tf_op jit(solution)/shard_map/ppermute | solution.py:49
  87.6 0.8 copy-start.4
  88.3 10.6 %collective-permute-start.8 = (bf16[1,1792,128]{2,1,0:T(8,128)(2,1)S(1)}, bf16[1,1792,128]{2,1,0:T(8,128)(2,1)S(1)}, u32[]{:S(2)}, u32[]{:S(2)}) collective-permute-start(bf16[1,1792,128]{2,1,0:T(8,128)(2,1)S(1)} %collective-permute-done.7), channel_id=1, source_target_pairs={{0,1},{1,2},{2,3},{3,4},{4,5},{5,6},{6,7},{7,8},{8,9},{9,10},{10,1... | collective-permute-start | bytes 1376264 | tf_op jit(solution)/shard_map/ppermute | solution.py:49
  98.9 0.8 copy-start.6
  99.7 10.6 %collective-permute-start.9 = (bf16[1,1792,128]{2,1,0:T(8,128)(2,1)S(1)}, bf16[1,1792,128]{2,1,0:T(8,128)(2,1)S(1)}, u32[]{:S(2)}, u32[]{:S(2)}) collective-permute-start(bf16[1,1792,128]{2,1,0:T(8,128)(2,1)S(1)} %collective-permute-done.8), channel_id=1, source_target_pairs={{0,1},{1,2},{2,3},{3,4},{4,5},{5,6},{6,7},{7,8},{8,9},{9,10},{10,1... | collective-permute-start | bytes 1376264 | tf_op jit(solution)/shard_map/ppermute | solution.py:49
  110.3 0.8 copy-start.8
  111.1 10.6 %collective-permute-start.10 = (bf16[1,1792,128]{2,1,0:T(8,128)(2,1)S(1)}, bf16[1,1792,128]{2,1,0:T(8,128)(2,1)S(1)}, u32[]{:S(2)}, u32[]{:S(2)}) collective-permute-start(bf16[1,1792,128]{2,1,0:T(8,128)(2,1)S(1)} %collective-permute-done.9), channel_id=1, source_target_pairs={{0,1},{1,2},{2,3},{3,4},{4,5},{5,6},{6,7},{7,8},{8,9},{9,10},{10,1... | collective-permute-start | bytes 1376264 | tf_op jit(solution)/shard_map/ppermute | solution.py:49
  121.7 0.8 copy-start.10
  122.5 10.6 %collective-permute-start.11 = (bf16[1,1792,128]{2,1,0:T(8,128)(2,1)S(1)}, bf16[1,1792,128]{2,1,0:T(8,128)(2,1)S(1)}, u32[]{:S(2)}, u32[]{:S(2)}) collective-permute-start(bf16[1,1792,128]{2,1,0:T(8,128)(2,1)S(1)} %collective-permute-done.10), channel_id=1, source_target_pairs={{0,1},{1,2},{2,3},{3,4},{4,5},{5,6},{6,7},{7,8},{8,9},{9,10},{10,1... | collective-permute-start | bytes 1376264 | tf_op jit(solution)/shard_map/ppermute | solution.py:49
  133.1 13.2 %copy-start.12 = (bf16[1,1792,128]{2,1,0:T(8,128)(2,1)}, bf16[1,1792,128]{2,1,0:T(8,128)(2,1)S(1)}, u32[]{:S(2)}) copy-start(bf16[1,1792,128]{2,1,0:T(8,128)(2,1)S(1)} %collective-permute-done.11) | copy-start | bytes 1376260
  133.1 13.1 %collective-permute-start.12 = (bf16[1,1792,128]{2,1,0:T(8,128)(2,1)S(1)}, bf16[1,1792,128]{2,1,0:T(8,128)(2,1)}, u32[]{:S(2)}, u32[]{:S(2)}) collective-permute-start(bf16[1,1792,128]{2,1,0:T(8,128)(2,1)S(1)} %collective-permute-done.11), channel_id=1, source_target_pairs={{0,1},{1,2},{2,3},{3,4},{4,5},{5,6},{6,7},{7,8},{8,9},{9,10},{10,1... | collective-permute-start | bytes 1376264 | tf_op jit(solution)/shard_map/ppermute | solution.py:49
  133.9 12.2 %all-to-all-start = ((s32[16,1,12]{2,1,0:T(1,128)}), s32[16,1,12]{2,1,0:T(1,128)S(1)}, u32[]{:S(2)}, u32[]{:S(2)}) async-start(s32[16,1,12]{2,1,0:T(1,128)} %bitcast.12), calls=%async_computation | async-start | bytes 16384 | tf_op jit(solution)/shard_map/all_to_all | solution.py:42
  146.2 13.5 %collective-permute-start.13 = (bf16[1,1792,128]{2,1,0:T(8,128)(2,1)}, bf16[1,1792,128]{2,1,0:T(8,128)(2,1)}, u32[]{:S(2)}, u32[]{:S(2)}) collective-permute-start(bf16[1,1792,128]{2,1,0:T(8,128)(2,1)} %collective-permute-done.12), channel_id=1, source_target_pairs={{0,1},{1,2},{2,3},{3,4},{4,5},{5,6},{6,7},{7,8},{8,9},{9,10},{10,1... | collective-permute-start | bytes 1376264 | tf_op jit(solution)/shard_map/ppermute | solution.py:49
  156.5 28.4 %copy-start.1 = (bf16[56,32,128]{2,1,0:T(8,128)(2,1)S(1)}, bf16[56,32,128]{2,1,0:T(8,128)(2,1)}, u32[]{:S(2)}) copy-start(bf16[56,32,128]{2,1,0:T(8,128)(2,1)} %param.6) | copy-start | bytes 1376260
  159.5 15.7 %copy-start.13 = (bf16[1,1792,128]{2,1,0:T(8,128)(2,1)S(1)}, bf16[1,1792,128]{2,1,0:T(8,128)(2,1)}, u32[]{:S(2)}) copy-start(bf16[1,1792,128]{2,1,0:T(8,128)(2,1)} %copy-done.12) | copy-start | bytes 1376260
  159.5 16.5 %copy-start.11 = (bf16[1,1792,128]{2,1,0:T(8,128)(2,1)S(1)}, bf16[1,1792,128]{2,1,0:T(8,128)(2,1)}, u32[]{:S(2)}) copy-start(bf16[1,1792,128]{2,1,0:T(8,128)(2,1)} %copy-done.10) | copy-start | bytes 1376260
  159.5 17.3 %copy-start.9 = (bf16[1,1792,128]{2,1,0:T(8,128)(2,1)S(1)}, bf16[1,1792,128]{2,1,0:T(8,128)(2,1)}, u32[]{:S(2)}) copy-start(bf16[1,1792,128]{2,1,0:T(8,128)(2,1)} %copy-done.8) | copy-start | bytes 1376260
  159.5 18.1 %copy-start.7 = (bf16[1,1792,128]{2,1,0:T(8,128)(2,1)S(1)}, bf16[1,1792,128]{2,1,0:T(8,128)(2,1)}, u32[]{:S(2)}) copy-start(bf16[1,1792,128]{2,1,0:T(8,128)(2,1)} %copy-done.6) | copy-start | bytes 1376260
  159.5 18.9 %copy-start.5 = (bf16[1,1792,128]{2,1,0:T(8,128)(2,1)S(1)}, bf16[1,1792,128]{2,1,0:T(8,128)(2,1)}, u32[]{:S(2)}) copy-start(bf16[1,1792,128]{2,1,0:T(8,128)(2,1)} %copy-done.4) | copy-start | bytes 1376260
  159.5 19.7 %copy-start.3 = (bf16[1,1792,128]{2,1,0:T(8,128)(2,1)S(1)}, bf16[1,1792,128]{2,1,0:T(8,128)(2,1)}, u32[]{:S(2)}) copy-start(bf16[1,1792,128]{2,1,0:T(8,128)(2,1)} %copy-done.2) | copy-start | bytes 1376260
  159.7 11.1 %collective-permute-start.14 = (bf16[1,1792,128]{2,1,0:T(8,128)(2,1)}, bf16[1,1792,128]{2,1,0:T(8,128)(2,1)S(1)}, u32[]{:S(2)}, u32[]{:S(2)}) collective-permute-start(bf16[1,1792,128]{2,1,0:T(8,128)(2,1)} %collective-permute-done.13), channel_id=1, source_target_pairs={{0,1},{1,2},{2,3},{3,4},{4,5},{5,6},{6,7},{7,8},{8,9},{9,10},{10,1... | collective-permute-start | bytes 1376264 | tf_op jit(solution)/shard_map/ppermute | solution.py:49
  207.5 37.3 %copy-start.15 = (s32[1,128]{1,0:T(1,128)S(1)}, s32[1,128]{1,0:T(1,128)}, u32[]{:S(2)}) copy-start(s32[1,128]{1,0:T(1,128)} %param.9) | copy-start | bytes 1540
  241.2 10.2 %all-to-all-start.1 = ((f32[16,1,672]{2,1,0:T(1,128)}), f32[16,1,672]{2,1,0:T(1,128)S(1)}, u32[]{:S(2)}, u32[]{:S(2)}) async-start(f32[16,1,672]{2,1,0:T(1,128)} %reshape.217), calls=%async_computation.1 | async-start | bytes 98304 | tf_op jit(solution)/shard_map/all_to_all | solution.py:64
  253.7 3.2 %copy-start.14 = (f32[56,128]{1,0:T(8,128)}, f32[56,128]{1,0:T(8,128)S(1)}, u32[]{:S(2)}) copy-start(f32[56,128]{1,0:T(8,128)S(1)} %copy.27) | copy-start | bytes 86020
